TPU v7x, 32 devices: a whole 2x2x4 slice. The times are simulated.
32 devices in a mesh: dp: 16 (over z, y, core), query: 2 (over x).
Axes of the slice: x: 2, y: 2, z: 4, core: 2. Of those that a mesh axis runs over, the one named last changes fastest.
Arguments:
- tokens: bfloat16 [2, 32, 128, 1280], P(None, ('dp', 'query')), may hold values from -6 to 6
- out_cotangent: bfloat16 [2, 32, 128, 1280], P(None, ('dp', 'query')), may hold values from -6 to 6
- qkv_weight: bfloat16 [1280, 3840], P('dp'), may hold values from -0.15625 to 0.15625
- out_weight: bfloat16 [1280, 1280], P('dp'), may hold values from -0.625 to 0.625
- up_weight: bfloat16 [1280, 5120], P('dp'), may hold values from -0.15625 to 0.15625
- down_weight: bfloat16 [5120, 1280], P('dp'), may hold values from -0.078125 to 0.078125
- attn_gain: bfloat16 [1280], P('dp'), may hold values from 0.5 to 1.5
- ffn_gain: bfloat16 [1280], P('dp'), may hold values from 0.5 to 1.5
- up_bias: bfloat16 [5120], P('dp'), may hold values from -3 to 3
- cell_weight: bfloat16 [1280, 5120], P('dp'), may hold values from -0.15625 to 0.15625
- gene_weight: bfloat16 [1280, 5120], P('dp'), may hold values from -0.15625 to 0.15625
- decoder_bias: bfloat16 [5120], P('dp'), may hold values from -3 to 3
- readout: bfloat16 [5120], P('dp'), may hold values from -0.15625 to 0.15625
- gene_embed: bfloat16 [2, 32, 384, 1280], P(None, ('dp', 'query')), may hold values from -6 to 6
- query_cell: int32 [2, 32, 384], P(None, ('dp', 'query')), may hold values from 0 to 1
- query_label: int32 [2, 32, 384], P(None, ('dp', 'query')), may hold values 0 or 1
- query_live: int32 [16, 2, 2], P('dp', None, 'query'), may hold values from 1 to 384, 480 in all within a row
Outputs:
- block_out: bfloat16 [2, 32, 128, 1280], P(None, ('dp', 'query'))
- grad_tokens: float32 [2, 32, 128, 1280], P(None, ('dp', 'query'))
- grad_qkv: float32 [1280, 3840], P('dp')
- grad_out: float32 [1280, 1280], P('dp')
- grad_up: float32 [1280, 5120], P('dp')
- grad_down: float32 [5120, 1280], P('dp')
- grad_attn_gain: float32 [1280], P('dp')
- grad_ffn_gain: float32 [1280], P('dp')
- grad_up_bias: float32 [5120], P('dp')
- grad_cell: float32 [1280, 5120], P('dp')
- grad_gene: float32 [1280, 5120], P('dp')
- grad_decoder_bias: float32 [5120], P('dp')
- grad_readout: float32 [5120], P('dp')
Inputs may be any that keep to these rules, and one draw needn't show every extreme that they name: `query_live`: the 2 devices of one dp index together hold 480 live rows in each micro-batch; a device's live rows are its first slots. `query_cell`: index of a cell within the query group of the row's device.
All inputs are finite; a program needn't handle non-finite values. No bound on the sum of `query_label` on one device may be relied on, other than what follows from the above.
Results may differ from a plain program's by a relative error of at most 0.02.
Values may be sent and summed in bfloat16 or wider, within the bound.
No kernel may reach another device: no remote copies, remote signals or barrier semaphores. Data moves between devices by JAX's collectives and lax.ppermute only.
A program may use at most 320 MiB of HBM per device.

v0:
```python
import jax
import jax.numpy as jnp
from jax import lax
from jax.sharding import PartitionSpec as P

D = 1280
HEADS = 20
HEAD = 64
highest = lax.Precision.HIGHEST
epsilon = 1e-05


def row_product(left, right):
    return lax.dot_general(
        left, right, (((0,), (0,)), ((), ())), preferred_element_type=jnp.float32
    )


def times_transpose(left, right):
    return lax.dot_general(
        left, right, (((1,), (1,)), ((), ())), preferred_element_type=jnp.float32
    )


def layer_stats(values):
    average = jnp.mean(values, axis=-1, keepdims=True)
    centred = values - average
    variance = jnp.mean(centred * centred, axis=-1, keepdims=True)
    inverse = lax.rsqrt(variance + epsilon)
    return (centred * inverse, inverse)


def norm_back(grad_scaled, gain, normal, inverse):
    grad_normal = grad_scaled * gain
    along_normal = jnp.mean(grad_normal * normal, axis=-1, keepdims=True)
    average = jnp.mean(grad_normal, axis=-1, keepdims=True)
    grad_values = inverse * (grad_normal - average - normal * along_normal)
    return (grad_values, jnp.sum(grad_scaled * normal, axis=0))


def encode(inputs, weights):
    qkv_weight, out_weight, up_weight, down_weight, attn_gain, ffn_gain, up_bias = weights
    length = inputs.shape[0]
    tokens_wide = inputs.astype(jnp.float32)
    norm_one, scale_one = layer_stats(tokens_wide)
    normed = (norm_one * attn_gain.astype(jnp.float32)).astype(jnp.bfloat16)
    projected = jnp.dot(normed, qkv_weight, preferred_element_type=jnp.float32).astype(jnp.bfloat16)
    projected = projected.reshape(length, 3, HEADS, HEAD)
    queries = projected[:, 0]
    key_heads = projected[:, 1]
    value_heads = projected[:, 2]
    scores = (
        jnp.einsum("qhd,khd->hqk", queries, key_heads, preferred_element_type=jnp.float32) * 0.125
    )
    row_max = jnp.max(scores, axis=-1, keepdims=True)
    shifted = jnp.exp(scores - row_max)
    row_total = jnp.sum(shifted, axis=-1, keepdims=True)
    attn_probs = (shifted / row_total).astype(jnp.bfloat16)
    logsum = row_max + jnp.log(row_total)
    mixed_heads = jnp.einsum(
        "hqk,khd->qhd", attn_probs, value_heads, preferred_element_type=jnp.float32
    )
    mixed_heads = mixed_heads.astype(jnp.bfloat16).reshape(length, D)
    hidden = tokens_wide + jnp.dot(mixed_heads, out_weight, preferred_element_type=jnp.float32)
    norm_two, scale_two = layer_stats(hidden)
    second = (norm_two * ffn_gain.astype(jnp.float32)).astype(jnp.bfloat16)
    up_proj = jnp.dot(second, up_weight, preferred_element_type=jnp.float32) + up_bias.astype(
        jnp.float32
    )
    active = jax.nn.gelu(up_proj, approximate=True).astype(jnp.bfloat16)
    output = hidden + jnp.dot(active, down_weight, preferred_element_type=jnp.float32)
    saved_state = (
        norm_one,
        scale_one,
        normed,
        queries,
        key_heads,
        value_heads,
        logsum,
        mixed_heads,
        norm_two,
        scale_two,
        second,
        up_proj,
        active,
    )
    return (output, saved_state)


def encode_back(grad_output, saved_state, weights):
    qkv_weight, out_weight, up_weight, down_weight, attn_gain, ffn_gain = weights
    (
        norm_one,
        scale_one,
        normed,
        queries,
        key_heads,
        value_heads,
        logsum,
        mixed_heads,
        norm_two,
        scale_two,
        second,
        up_proj,
        active,
    ) = saved_state
    length = grad_output.shape[0]
    grad_branch = grad_output.astype(jnp.bfloat16)
    grad_down = row_product(active, grad_branch)
    grad_active = times_transpose(grad_branch, down_weight)
    gelu_back = jax.vjp(lambda inner_values: jax.nn.gelu(inner_values, approximate=True), up_proj)[
        1
    ]
    grad_up_proj = gelu_back(grad_active)[0].astype(jnp.bfloat16)
    grad_up = row_product(second, grad_up_proj)
    grad_up_bias = jnp.sum(grad_up_proj.astype(jnp.float32), axis=0)
    grad_second = times_transpose(grad_up_proj, up_weight)
    grad_hidden_norm, grad_ffn_gain = norm_back(
        grad_second, ffn_gain.astype(jnp.float32), norm_two, scale_two
    )
    grad_hidden = grad_output + grad_hidden_norm
    grad_attn = grad_hidden.astype(jnp.bfloat16)
    grad_out = row_product(mixed_heads, grad_attn)
    grad_mixed = (
        times_transpose(grad_attn, out_weight).astype(jnp.bfloat16).reshape(length, HEADS, HEAD)
    )
    scores = (
        jnp.einsum("qhd,khd->hqk", queries, key_heads, preferred_element_type=jnp.float32) * 0.125
    )
    attn_probs = jnp.exp(scores - logsum)
    probs_low = attn_probs.astype(jnp.bfloat16)
    grad_values = jnp.einsum(
        "hqk,qhd->khd", probs_low, grad_mixed, preferred_element_type=jnp.float32
    )
    grad_probs = jnp.einsum(
        "qhd,khd->hqk", grad_mixed, value_heads, preferred_element_type=jnp.float32
    )
    along_probs = jnp.sum(grad_probs * attn_probs, axis=-1, keepdims=True)
    grad_scores = (attn_probs * (grad_probs - along_probs) * 0.125).astype(jnp.bfloat16)
    grad_queries = jnp.einsum(
        "hqk,khd->qhd", grad_scores, key_heads, preferred_element_type=jnp.float32
    )
    grad_keys = jnp.einsum("hqk,qhd->khd", grad_scores, queries, preferred_element_type=jnp.float32)
    grad_projected = (
        jnp.stack([grad_queries, grad_keys, grad_values], axis=1)
        .astype(jnp.bfloat16)
        .reshape(length, 3 * D)
    )
    grad_qkv = row_product(normed, grad_projected)
    grad_normed = times_transpose(grad_projected, qkv_weight)
    grad_input_norm, grad_attn_gain = norm_back(
        grad_normed, attn_gain.astype(jnp.float32), norm_one, scale_one
    )
    grad_input = grad_hidden + grad_input_norm
    return (
        (grad_qkv, grad_out, grad_up, grad_down, grad_attn_gain, grad_ffn_gain, grad_up_bias),
        grad_input,
    )


def decode(summary_all, weights, gene_rows, cell_ids, labels, live_count):
    cell_weight, gene_weight, decoder_bias, readout = weights
    group_size = summary_all.shape[0]
    slot_count = gene_rows.shape[0]
    cell_part = jnp.dot(summary_all, cell_weight, preferred_element_type=jnp.float32)
    onehot = (cell_ids[:, None] == jnp.arange(group_size, dtype=jnp.int32)[None, :]).astype(
        jnp.float32
    )
    picked = jnp.dot(onehot, cell_part, precision=highest)
    pre_act = (
        picked
        + jnp.dot(gene_rows, gene_weight, preferred_element_type=jnp.float32)
        + decoder_bias.astype(jnp.float32)
    )
    activity, silu_back = jax.vjp(jax.nn.silu, pre_act)
    read_wide = readout.astype(jnp.float32)
    logits = jnp.sum(activity * read_wide[None, :], axis=-1)
    live_rows = (jnp.arange(slot_count, dtype=jnp.int32) < live_count).astype(jnp.float32)
    grad_logits = live_rows * (jax.nn.sigmoid(logits) - labels.astype(jnp.float32))
    grad_readout = jnp.sum(grad_logits[:, None] * activity, axis=0)
    grad_pre = silu_back(grad_logits[:, None] * read_wide[None, :])[0].astype(jnp.bfloat16)
    grad_pre_wide = grad_pre.astype(jnp.float32)
    grad_decoder_bias = jnp.sum(grad_pre_wide, axis=0)
    grad_gene = row_product(gene_rows, grad_pre)
    grad_cellproj = lax.dot_general(
        onehot, grad_pre_wide, (((0,), (0,)), ((), ())), precision=highest
    )
    grad_cell = lax.dot_general(
        summary_all.astype(jnp.float32), grad_cellproj, (((0,), (0,)), ((), ())), precision=highest
    )
    grad_summary = lax.dot_general(
        grad_cellproj, cell_weight.astype(jnp.float32), (((1,), (1,)), ((), ())), precision=highest
    )
    return ((grad_cell, grad_gene, grad_decoder_bias, grad_readout), grad_summary)


def shards(
    tokens,
    out_cotangent,
    qkv_weight,
    out_weight,
    up_weight,
    down_weight,
    attn_gain,
    ffn_gain,
    up_bias,
    cell_weight,
    gene_weight,
    decoder_bias,
    readout,
    gene_embed,
    query_cell,
    query_label,
    query_live,
):
    micro_count = tokens.shape[0]
    outputs = []
    input_grads = []
    totals = None
    for micro_index in range(micro_count):
        gathered = (
            lax.all_gather(qkv_weight, "dp", axis=0, tiled=True),
            lax.all_gather(out_weight, "dp", axis=0, tiled=True),
            lax.all_gather(up_weight, "dp", axis=0, tiled=True),
            lax.all_gather(down_weight, "dp", axis=0, tiled=True),
            lax.all_gather(attn_gain, "dp", axis=0, tiled=True),
            lax.all_gather(ffn_gain, "dp", axis=0, tiled=True),
            lax.all_gather(up_bias, "dp", axis=0, tiled=True),
            lax.all_gather(cell_weight, "dp", axis=0, tiled=True),
            lax.all_gather(gene_weight, "dp", axis=0, tiled=True),
            lax.all_gather(decoder_bias, "dp", axis=0, tiled=True),
            lax.all_gather(readout, "dp", axis=0, tiled=True),
        )
        output, saved_state = encode(tokens[micro_index, 0], gathered[:7])
        outputs.append(output.astype(jnp.bfloat16))
        summary_all = lax.all_gather(output[0:1].astype(jnp.bfloat16), "query", axis=0, tiled=True)
        decoder_grads, grad_summary = decode(
            summary_all,
            gathered[7:],
            gene_embed[micro_index, 0],
            query_cell[micro_index, 0],
            query_label[micro_index, 0],
            query_live[0, micro_index, 0],
        )
        grad_own = lax.psum_scatter(
            grad_summary.astype(jnp.bfloat16), "query", scatter_dimension=0, tiled=True
        ).astype(jnp.float32)
        grad_output = out_cotangent[micro_index, 0].astype(jnp.float32)
        grad_output = grad_output.at[0:1].add(grad_own)
        back_weights = (
            lax.all_gather(qkv_weight, "dp", axis=0, tiled=True),
            lax.all_gather(out_weight, "dp", axis=0, tiled=True),
            lax.all_gather(up_weight, "dp", axis=0, tiled=True),
            lax.all_gather(down_weight, "dp", axis=0, tiled=True),
            lax.all_gather(attn_gain, "dp", axis=0, tiled=True),
            lax.all_gather(ffn_gain, "dp", axis=0, tiled=True),
        )
        encoder_grads, grad_input = encode_back(grad_output, saved_state, back_weights)
        input_grads.append(grad_input)
        step_grads = encoder_grads + decoder_grads
        if micro_index == 0:
            totals = tuple(step_grads)
        else:
            totals = tuple((earlier + later for earlier, later in zip(totals, step_grads)))
    owned = (
        lax.psum_scatter(
            totals[0].astype(jnp.bfloat16), "dp", scatter_dimension=0, tiled=True
        ).astype(jnp.float32),
        lax.psum_scatter(
            totals[1].astype(jnp.bfloat16), "dp", scatter_dimension=0, tiled=True
        ).astype(jnp.float32),
        lax.psum_scatter(
            totals[2].astype(jnp.bfloat16), "dp", scatter_dimension=0, tiled=True
        ).astype(jnp.float32),
        lax.psum_scatter(
            totals[3].astype(jnp.bfloat16), "dp", scatter_dimension=0, tiled=True
        ).astype(jnp.float32),
        lax.psum_scatter(
            totals[4].astype(jnp.bfloat16), "dp", scatter_dimension=0, tiled=True
        ).astype(jnp.float32),
        lax.psum_scatter(
            totals[5].astype(jnp.bfloat16), "dp", scatter_dimension=0, tiled=True
        ).astype(jnp.float32),
        lax.psum_scatter(
            totals[6].astype(jnp.bfloat16), "dp", scatter_dimension=0, tiled=True
        ).astype(jnp.float32),
        lax.psum_scatter(
            totals[7].astype(jnp.bfloat16), "dp", scatter_dimension=0, tiled=True
        ).astype(jnp.float32),
        lax.psum_scatter(
            totals[8].astype(jnp.bfloat16), "dp", scatter_dimension=0, tiled=True
        ).astype(jnp.float32),
        lax.psum_scatter(
            totals[9].astype(jnp.bfloat16), "dp", scatter_dimension=0, tiled=True
        ).astype(jnp.float32),
        lax.psum_scatter(
            totals[10].astype(jnp.bfloat16), "dp", scatter_dimension=0, tiled=True
        ).astype(jnp.float32),
    )
    totals = (
        lax.psum(owned[0].astype(jnp.bfloat16), "query").astype(jnp.float32),
        lax.psum(owned[1].astype(jnp.bfloat16), "query").astype(jnp.float32),
        lax.psum(owned[2].astype(jnp.bfloat16), "query").astype(jnp.float32),
        lax.psum(owned[3].astype(jnp.bfloat16), "query").astype(jnp.float32),
        lax.psum(owned[4].astype(jnp.bfloat16), "query").astype(jnp.float32),
        lax.psum(owned[5].astype(jnp.bfloat16), "query").astype(jnp.float32),
        lax.psum(owned[6].astype(jnp.bfloat16), "query").astype(jnp.float32),
        lax.psum(owned[7].astype(jnp.bfloat16), "query").astype(jnp.float32),
        lax.psum(owned[8].astype(jnp.bfloat16), "query").astype(jnp.float32),
        lax.psum(owned[9].astype(jnp.bfloat16), "query").astype(jnp.float32),
        lax.psum(owned[10].astype(jnp.bfloat16), "query").astype(jnp.float32),
    )
    block_out = jnp.stack(outputs, axis=0)[:, None]
    grad_tokens = jnp.stack(input_grads, axis=0)[:, None]
    return (
        block_out,
        grad_tokens,
        totals[0],
        totals[1],
        totals[2],
        totals[3],
        totals[4],
        totals[5],
        totals[6],
        totals[7],
        totals[8],
        totals[9],
        totals[10],
    )


def solution(mesh):
    placed = (
        P(None, ("dp", "query"), None, None),
        P(None, ("dp", "query"), None, None),
        P("dp", None),
        P("dp", None),
        P("dp", None),
        P("dp", None),
        P("dp"),
        P("dp"),
        P("dp"),
        P("dp", None),
        P("dp", None),
        P("dp"),
        P("dp"),
        P(None, ("dp", "query"), None, None),
        P(None, ("dp", "query"), None),
        P(None, ("dp", "query"), None),
        P("dp", None, "query"),
    )
    return jax.shard_map(
        shards,
        mesh=mesh,
        in_specs=placed,
        out_specs=(
            P(None, ("dp", "query"), None, None),
            P(None, ("dp", "query"), None, None),
            P("dp", None),
            P("dp", None),
            P("dp", None),
            P("dp", None),
            P("dp"),
            P("dp"),
            P("dp"),
            P("dp", None),
            P("dp", None),
            P("dp"),
            P("dp"),
        ),
        check_vma=False,
    )
```

profile of v0, /device:TPU:0, one launch (start us, length us, event | category | flops | bytes accessed | tf_op | source)
XLA Modules:
  0.0 1549.0 jit_solution(1948422574728645002)
XLA Ops:
  14.5 65.3 %all-reduce.13 = (bf16[1280]{0:T(1024)(128)(2,1)S(1)}, bf16[5120]{0:T(1024)(128)(2,1)S(1)}, bf16[1280]{0:T(1024)(128)(2,1)S(1)}, bf16[5120]{0:T(1024)(128)(2,1)S(1)}, bf16[5120]{0:T(1024)(128)(2,1)S(1)}) all-reduce(bf16[1280]{0:T(1024)(128)(2,1)S(1)} %dynamic-update-slice.6, ...), channel_id=1, replica_groups=mesh['dp'=16,'query'=2] {'dp'}, use_global_device_ids=true, to_apply=%add | all-reduce | flops 17920 | bytes 71680
  81.0 16.6 %all-gather.9.cloned.1.call-done = bf16[1280,3840]{1,0:T(8,128)(2,1)} async-done(((bf16[80,3840]{1,0:T(8,128)(2,1)}), bf16[1280,3840]{1,0:T(8,128)(2,1)}) %all-gather.9.cloned.1.call-update) | async-done | bytes 9830416 | tf_op jit(solution)/shard_map/all_gather | solution.py:222
  97.6 5.3 convolution_convert_fusion
  103.7 5.9 convolution_convert_fusion.1
  112.9 31.2 %all-gather.11.cloned.1.call-done = bf16[1280,1280]{1,0:T(8,128)(2,1)} async-done(((bf16[80,1280]{1,0:T(8,128)(2,1)}), bf16[1280,1280]{1,0:T(8,128)(2,1)}) %all-gather.11.cloned.1.call-update) | async-done | bytes 3276816 | tf_op jit(solution)/shard_map/all_gather | solution.py:223
  151.0 98.3 %all-gather.13.cloned.1.call-done = bf16[1280,5120]{1,0:T(8,128)(2,1)} async-done(((bf16[80,5120]{1,0:T(8,128)(2,1)}), bf16[1280,5120]{1,0:T(8,128)(2,1)}) %all-gather.13.cloned.1.call-update) | async-done | bytes 13107216 | tf_op jit(solution)/shard_map/all_gather | solution.py:224
  249.3 8.2 convolution_add_fusion.1
  257.5 96.1 %all-gather.15.cloned.1.call-done = bf16[5120,1280]{1,0:T(8,128)(2,1)} async-done(((bf16[320,1280]{1,0:T(8,128)(2,1)}), bf16[5120,1280]{1,0:T(8,128)(2,1)}) %all-gather.15.cloned.1.call-update) | async-done | bytes 13107216 | tf_op jit(solution)/shard_map/all_gather | solution.py:225
  353.6 8.0 fusion.27
  361.6 4.7 all-gather.1
  370.8 4.4 all-gather
  375.1 82.8 %all-gather.17.cloned.1.call-done = bf16[1280,5120]{1,0:T(8,128)(2,1)} async-done(((bf16[80,5120]{1,0:T(8,128)(2,1)}), bf16[1280,5120]{1,0:T(8,128)(2,1)}) %all-gather.17.cloned.1.call-update) | async-done | bytes 13107216 | tf_op jit(solution)/shard_map/all_gather | solution.py:229
  457.9 6.5 fusion.165
  464.5 97.8 %all-gather.19.cloned.1.call-done = bf16[1280,5120]{1,0:T(8,128)(2,1)} async-done(((bf16[80,5120]{1,0:T(8,128)(2,1)}), bf16[1280,5120]{1,0:T(8,128)(2,1)}) %all-gather.19.cloned.1.call-update) | async-done | bytes 13107216 | tf_op jit(solution)/shard_map/all_gather | solution.py:230
  562.3 10.5 fusion.49
  572.8 6.2 add_add_fusion
  579.1 12.6 fusion.53
  593.6 9.9 multiply_reduce_fusion.3
  604.8 11.1 convert_reduce_fusion.1
  615.9 12.7 fusion.51
  628.6 16.2 %fusion.2 = bf16[1280,5120]{0,1:T(8,128)(2,1)} fusion(f32[5120,1280]{1,0:T(8,128)} %fusion.51, bf16[384,5120]{1,0:T(8,128)(2,1)} %get-tuple-element.137, bf16[2,1,384,1280]{3,2,1,0:T(8,128)(2,1)} %param.34), kind=kOutput, calls=%fused_computation.7 | convolution fusion | flops 5046272000 | bytes 44236800 | tf_op jit(solution)/shard_map/dot_general | solution.py:14
  644.8 17.6 %copy.89 = bf16[1280,5120]{1,0:T(8,128)(2,1)} copy(bf16[1280,5120]{0,1:T(8,128)(2,1)} %fusion.2) | data formatting | bytes 26214400
  670.4 14.2 convolution_convert_fusion.5
  684.5 13.5 convolution_convert_fusion.4
  698.0 8.3 all-reduce.15
  708.9 11.2 convert_reduce_fusion.3
  720.1 10.6 multiply_reduce_fusion.7
  730.7 9.7 convert_reduce_fusion.2
  740.5 10.3 multiply_reduce_fusion.6
  771.7 3.2 convolution_bitcast_fusion.4
  777.3 3.1 convolution_bitcast_fusion.2
  786.1 8.3 fusion.116
  794.5 11.1 add_convert_fusion.4
  806.7 12.7 fusion.185
  819.5 15.7 %add_convert_fusion.3 = bf16[1280,5120]{1,0:T(8,128)(2,1)} fusion(f32[1280,5120]{1,0:T(8,128)} %fusion.185, bf16[128,5120]{1,0:T(8,128)(2,1)} %copy-done.26, f32[128,1280]{1,0:T(8,128)S(1)} %copy-done.6, f32[128]{0:T(128)S(1)} %copy-done.75, f32[128]{0:T(128)S(1)} %copy-done.70, f32[1280]{0:T(1024)S(1)} %convert_element_type.331), kind=kOutput, calls=%fused_computation.5 | convolution fusion | flops 1691484160 | bytes 41293824 | tf_op jit(solution)/shard_map/dot_general | solution.py:14
  836.3 12.8 fusion.146
  849.1 16.3 %add_convert_fusion.2 = bf16[5120,1280]{1,0:T(8,128)(2,1)} fusion(f32[5120,1280]{1,0:T(8,128)} %fusion.146, f32[128,1280]{1,0:T(8,128)S(1)} %copy-done.22, f32[128,5120]{1,0:T(8,128)} %convolution_add_fusion.1), kind=kOutput, calls=%fused_computation.4 | convolution fusion | flops 1696890880 | bytes 42598400 | tf_op jit(solution)/shard_map/dot_general | solution.py:14
  866.1 13.9 fusion.167
  880.0 19.8 %add_convert_fusion.1 = bf16[1280,5120]{1,0:T(8,128)(2,1)} fusion(f32[1280,5120]{1,0:T(8,128)} %fusion.167, f32[2,5120]{1,0:T(2,128)S(1)} %fusion.134, bf16[2,1,1280]{2,1,0:T(2,128)(2,1)S(1)} %copy-done.61), kind=kOutput, calls=%fused_computation.3 | convolution fusion | flops 170393600 | bytes 39367680 | tf_op jit(solution)/shard_map/dot_general | solution.py:188
  903.5 83.3 %reduce-scatter.9.cloned.1.call-done = bf16[80,3840]{1,0:T(8,128)(2,1)} async-done(((bf16[1280,3840]{1,0:T(8,128)(2,1)}), bf16[80,3840]{1,0:T(8,128)(2,1)}) %reduce-scatter.9.cloned.1.call-update) | async-done | bytes 614416 | tf_op jit(solution)/shard_map/reduce_scatter | solution.py:266
  986.8 142.1 %reduce-scatter.13.cloned.1.call-done = bf16[80,5120]{1,0:T(8,128)(2,1)} async-done(((bf16[1280,5120]{1,0:T(8,128)(2,1)}), bf16[80,5120]{1,0:T(8,128)(2,1)}) %reduce-scatter.13.cloned.1.call-update) | async-done | bytes 819216 | tf_op jit(solution)/shard_map/reduce_scatter | solution.py:272
  1128.9 142.2 %reduce-scatter.15.cloned.1.call-done = bf16[320,1280]{1,0:T(8,128)(2,1)} async-done(((bf16[5120,1280]{1,0:T(8,128)(2,1)}), bf16[320,1280]{1,0:T(8,128)(2,1)}) %reduce-scatter.15.cloned.1.call-update) | async-done | bytes 819216 | tf_op jit(solution)/shard_map/reduce_scatter | solution.py:275
  1271.1 141.5 %reduce-scatter.17.cloned.1.call-done = bf16[80,5120]{1,0:T(8,128)(2,1)} async-done(((bf16[1280,5120]{1,0:T(8,128)(2,1)}), bf16[80,5120]{1,0:T(8,128)(2,1)}) %reduce-scatter.17.cloned.1.call-update) | async-done | bytes 819216 | tf_op jit(solution)/shard_map/reduce_scatter | solution.py:287
  1412.6 7.2 fusion.194
  1419.9 8.4 fusion.81
  1428.5 59.6 %all-reduce.12 = (bf16[1280]{0:T(1024)(128)(2,1)S(1)}, bf16[1280]{0:T(1024)(128)(2,1)S(1)}, bf16[5120]{0:T(1024)(128)(2,1)S(1)}, bf16[5120]{0:T(1024)(128)(2,1)S(1)}, bf16[5120]{0:T(1024)(128)(2,1)S(1)}) all-reduce(bf16[1280]{0:T(1024)(128)(2,1)S(1)} %add_convert_fusion.9, ...), channel_id=8, replica_groups=mesh['dp'=16,'query'=2] {'dp'}, use_global_device_ids=true, to_apply=%region_36.37.clone | all-reduce | flops 17920 | bytes 71680
  1488.5 5.0 all-reduce.14
  1499.9 33.9 %all-reduce.19.cloned.1.call-done = (bf16[80,5120]{0,1:T(8,128)(2,1)}, bf16[80,3840]{1,0:T(8,128)(2,1)}, bf16[80,1280]{1,0:T(8,128)(2,1)}, bf16[80,5120]{1,0:T(8...) async-done(((bf16[80,5120]{0,1:T(8,128)(2,1)}, bf16[80,3840]{1,0:T(8,128)(2,1)}, bf16[80,1280]{1,0:T(8,128)(2,1)}, bf16[80,5120]{1,0:T(8,128)(2,1)}, ...) | async-done | bytes 4096016 | tf_op jit(solution)/shard_map/psum | solution.py:309
  (335 shorter events, 85.2 us)
Async XLA Ops:
  7.2 72.5 %copy-start.85 = (s32[1,2,1]{1,2,0:T(1,128)S(1)}, s32[1,2,1]{1,2,0:T(1,128)}, u32[]{:S(2)}) copy-start(s32[1,2,1]{1,2,0:T(1,128)} %param.37) | copy-start | bytes 28
  7.3 73.1 %copy-start.82 = (s32[2,1,384]{2,1,0:T(1,128)S(1)}, s32[2,1,384]{2,1,0:T(1,128)}, u32[]{:S(2)}) copy-start(s32[2,1,384]{2,1,0:T(1,128)} %param.35) | copy-start | bytes 9220
  7.3 73.1 %copy-start.83 = (s32[2,1,384]{2,1,0:T(1,128)S(1)}, s32[2,1,384]{2,1,0:T(1,128)}, u32[]{:S(2)}) copy-start(s32[2,1,384]{2,1,0:T(1,128)} %param.36) | copy-start | bytes 9220
  7.3 73.2 %copy-start.7 = (bf16[2,1,128,1280]{3,2,1,0:T(8,128)(2,1)S(1)}, bf16[2,1,128,1280]{3,2,1,0:T(8,128)(2,1)}, u32[]{:S(2)}) copy-start(bf16[2,1,128,1280]{3,2,1,0:T(8,128)(2,1)} %param.21) | copy-start | bytes 1966084
  7.3 90.3 %all-gather.9.cloned.1.call-start = ((), (), s32[]{:S(2)}) async-start(), calls=%async_computation.6 | async-start | bytes 10444800 | tf_op jit(solution)/shard_map/all_gather | solution.py:222
  8.0 136.1 %all-gather.11.cloned.1.call-start = ((), (), s32[]{:S(2)}) async-start(), calls=%async_computation.7 | async-start | bytes 3481600 | tf_op jit(solution)/shard_map/all_gather | solution.py:223
  8.8 240.5 %all-gather.13.cloned.1.call-start = ((), (), s32[]{:S(2)}) async-start(), calls=%async_computation.8 | async-start | bytes 13926400 | tf_op jit(solution)/shard_map/all_gather | solution.py:224
  9.5 344.1 %all-gather.15.cloned.1.call-start = ((), (), s32[]{:S(2)}) async-start(), calls=%async_computation.9 | async-start | bytes 13926400 | tf_op jit(solution)/shard_map/all_gather | solution.py:225
  10.1 447.9 %all-gather.17.cloned.1.call-start = ((), (), s32[]{:S(2)}) async-start(), calls=%async_computation.10 | async-start | bytes 13926400 | tf_op jit(solution)/shard_map/all_gather | solution.py:229
  10.7 551.6 %all-gather.19.cloned.1.call-start = ((), (), s32[]{:S(2)}) async-start(), calls=%async_computation.11 | async-start | bytes 13926400 | tf_op jit(solution)/shard_map/all_gather | solution.py:230
  11.2 889.9 %reduce-scatter.19.cloned.1.call-start = ((), (), s32[]{:S(2)}) async-start(), calls=%async_computation.17 | async-start | bytes 13926400
  79.8 23.9 %copy-start.43 = (f32[1280]{0:T(1024)}, f32[1280]{0:T(1024)S(1)}, u32[]{:S(2)}) copy-start(f32[1280]{0:T(1024)S(1)} %convert_element_type.325) | copy-start | bytes 15364
  80.6 22.3 %copy-start.76 = (f32[128]{0:T(128)}, f32[128]{0:T(128)S(1)}, u32[]{:S(2)}) copy-start(f32[128]{0:T(128)S(1)} %get-tuple-element.159) | copy-start | bytes 1540
  80.6 23.0 %copy-start.71 = (f32[128]{0:T(128)}, f32[128]{0:T(128)S(1)}, u32[]{:S(2)}) copy-start(f32[128]{0:T(128)S(1)} %get-tuple-element.160) | copy-start | bytes 1540
  81.0 22.0 %copy-start.80 = (f32[128]{0:T(128)}, f32[128]{0:T(128)S(1)}, u32[]{:S(2)}) copy-start(f32[128]{0:T(128)S(1)} %add_rsqrt_fusion.1) | copy-start | bytes 1540
  81.0 22.6 %copy-start.78 = (f32[128]{0:T(128)}, f32[128]{0:T(128)S(1)}, u32[]{:S(2)}) copy-start(f32[128]{0:T(128)S(1)} %add_rsqrt_fusion.3) | copy-start | bytes 1540
  112.9 34.1 %copy-start.38 = (bf16[20,64,128]{2,1,0:T(8,128)(2,1)}, bf16[20,64,128]{2,1,0:T(8,128)(2,1)S(1)}, u32[]{:S(2)}) copy-start(bf16[20,64,128]{2,1,0:T(8,128)(2,1)S(1)} %convolution_convert_fusion.6) | copy-start | bytes 983044
  146.8 605.1 %copy-start.5 = (f32[128,1280]{1,0:T(8,128)}, f32[128,1280]{1,0:T(8,128)S(1)}, u32[]{:S(2)}) copy-start(f32[128,1280]{1,0:T(8,128)S(1)} %get-tuple-element.146) | copy-start | bytes 1966084
  146.8 102.5 %copy-start.69 = (f32[128]{0:T(128)}, f32[128]{0:T(128)S(1)}, u32[]{:S(2)}) copy-start(f32[128]{0:T(128)S(1)} %broadcast_multiply_fusion.8) | copy-start | bytes 1540
  150.7 589.7 %copy-start.9 = (f32[128,1280]{1,0:T(8,128)}, f32[128,1280]{1,0:T(8,128)S(1)}, u32[]{:S(2)}) copy-start(f32[128,1280]{1,0:T(8,128)S(1)} %get-tuple-element.150) | copy-start | bytes 1966084
  151.0 106.5 %copy-start.74 = (f32[128]{0:T(128)}, f32[128]{0:T(128)S(1)}, u32[]{:S(2)}) copy-start(f32[128]{0:T(128)S(1)} %add_rsqrt_fusion) | copy-start | bytes 1540
  353.6 12.7 copy-start
  353.6 14.7 slice-start.4
  353.6 14.7 slice-start.5
  353.6 14.7 slice-start.6
  366.3 91.6 %copy-start.60 = (bf16[2,1,1280]{2,1,0:T(2,128)(2,1)}, bf16[2,1,1280]{2,1,0:T(2,128)(2,1)S(1)}, u32[]{:S(2)}) copy-start(bf16[2,1,1280]{2,1,0:T(2,128)(2,1)S(1)} %all-gather.1) | copy-start | bytes 15364
  370.8 93.7 %copy-start.47 = (bf16[128,1280]{1,0:T(8,128)(2,1)}, bf16[128,1280]{1,0:T(8,128)(2,1)S(1)}, u32[]{:S(2)}) copy-start(bf16[128,1280]{1,0:T(8,128)(2,1)S(1)} %fusion.26) | copy-start | bytes 983044
  375.1 216.6 %copy-start.62 = (bf16[2,1,1280]{2,1,0:T(2,128)(2,1)}, bf16[2,1,1280]{2,1,0:T(2,128)(2,1)S(1)}, u32[]{:S(2)}) copy-start(bf16[2,1,1280]{2,1,0:T(2,128)(2,1)S(1)} %all-gather) | copy-start | bytes 15364
  572.8 18.9 %slice-start = ((s8[13107200]{0:T(1024)(128)(4,1)}), s8[4194304]{0:T(1024)(128)(4,1)S(1)}, s32[]{:S(2)}) async-start(s8[13107200]{0:T(1024)(128)(4,1)} %bitcast.251), calls=%async_computation.19 | async-start | bytes 8388608
  572.8 18.9 %slice-start.1 = ((s8[13107200]{0:T(1024)(128)(4,1)}), s8[4194304]{0:T(1024)(128)(4,1)S(1)}, s32[]{:S(2)}) async-start(s8[13107200]{0:T(1024)(128)(4,1)} %bitcast.251), calls=%async_computation.20 | async-start | bytes 8388608
  579.1 12.7 slice-start.2
  579.1 12.7 slice-start.3
  615.9 12.7 copy-start.4
  662.5 241.1 %reduce-scatter.11.cloned.1.call-start = ((), (), s32[]{:S(2)}) async-start(), calls=%async_computation.13 | async-start | bytes 3481600 | tf_op jit(solution)/shard_map/reduce_scatter | solution.py:269
  707.9 44.0 %copy-start.21 = (f32[128,1280]{1,0:T(8,128)}, f32[128,1280]{1,0:T(8,128)S(1)}, u32[]{:S(2)}) copy-start(f32[128,1280]{1,0:T(8,128)S(1)} %scatter-add.9) | copy-start | bytes 1966084
  708.9 31.6 %copy-start.23 = (f32[128,1280]{1,0:T(8,128)}, f32[128,1280]{1,0:T(8,128)S(1)}, u32[]{:S(2)}) copy-start(f32[128,1280]{1,0:T(8,128)S(1)} %scatter-add.6) | copy-start | bytes 1966084
  755.8 231.0 %reduce-scatter.9.cloned.1.call-start = ((), (), s32[]{:S(2)}) async-start(), calls=%async_computation.12 | async-start | bytes 10444800 | tf_op jit(solution)/shard_map/reduce_scatter | solution.py:266
  805.6 13.8 copy-start.6
  805.7 323.3 %reduce-scatter.13.cloned.1.call-start = ((), (), s32[]{:S(2)}) async-start(), calls=%async_computation.14 | async-start | bytes 13926400 | tf_op jit(solution)/shard_map/reduce_scatter | solution.py:272
  835.2 13.9 copy-start.22
  835.2 435.9 %reduce-scatter.15.cloned.1.call-start = ((), (), s32[]{:S(2)}) async-start(), calls=%async_computation.15 | async-start | bytes 13926400 | tf_op jit(solution)/shard_map/reduce_scatter | solution.py:275
  865.4 14.6 copy-start.61
  865.4 547.1 %reduce-scatter.17.cloned.1.call-start = ((), (), s32[]{:S(2)}) async-start(), calls=%async_computation.16 | async-start | bytes 13926400 | tf_op jit(solution)/shard_map/reduce_scatter | solution.py:287
  899.8 633.9 %all-reduce.19.cloned.1.call-start = ((), (), s32[]{:S(2)}) async-start(), calls=%async_computation.18 | async-start | bytes 9175040 | tf_op jit(solution)/shard_map/psum | solution.py:309
  1419.9 76.4 %copy-start.46 = (bf16[128,1280]{1,0:T(8,128)(2,1)S(1)}, bf16[128,1280]{1,0:T(8,128)(2,1)}, u32[]{:S(2)}) copy-start(bf16[128,1280]{1,0:T(8,128)(2,1)} %copy-done.45) | copy-start | bytes 983044
  1419.9 76.4 %copy-start.48 = (bf16[128,1280]{1,0:T(8,128)(2,1)S(1)}, bf16[128,1280]{1,0:T(8,128)(2,1)}, u32[]{:S(2)}) copy-start(bf16[128,1280]{1,0:T(8,128)(2,1)} %copy-done.47) | copy-start | bytes 983044
  1419.9 77.3 %copy-start.18 = (f32[128,1280]{1,0:T(8,128)S(1)}, f32[128,1280]{1,0:T(8,128)}, u32[]{:S(2)}) copy-start(f32[128,1280]{1,0:T(8,128)} %copy-done.17) | copy-start | bytes 1966084
  1419.9 77.2 %copy-start.20 = (f32[128,1280]{1,0:T(8,128)S(1)}, f32[128,1280]{1,0:T(8,128)}, u32[]{:S(2)}) copy-start(f32[128,1280]{1,0:T(8,128)} %copy-done.19) | copy-start | bytes 1966084
  (65 other events, 293.5 us)
Sparse Core Ops, SparseCore 0:
  10.4 87.1 all-gather.8
  99.9 44.1 all-gather.10
  146.4 102.8 all-gather.12
  251.4 102.1 all-gather.14
  355.7 102.1 all-gather.16
  460.1 102.1 all-gather.18
  662.6 136.5 reduce-scatter.18
  803.4 65.9 reduce-scatter.10
  873.6 113.2 reduce-scatter.8
  990.8 138.1 reduce-scatter.12
  1133.6 137.4 reduce-scatter.14
  1275.1 137.4 reduce-scatter.16
  1416.4 117.3 all-reduce.18
where the time goes:
time: 1560 us; the launch traced here: 1550 us
  waiting for transfers between devices  969 us (62%)
  matrix products  339 us (22%)
  blocking collectives  147 us (9%)
  local copies, waits for them, and re-layouts  41 us (3%)
  other arithmetic  33.2 us (2%)
  between operations  18 us (1%)
    reduce_scatter x1, waiting for transfers between devices, shards(): lax.psum_scatter(totals[3].astype(jnp.bfloat16), 'dp', scatter_dimension=...  142 us
    reduce_scatter x1, waiting for transfers between devices, shards(): lax.psum_scatter(totals[2].astype(jnp.bfloat16), 'dp', scatter_dimension=...  142 us
    reduce_scatter x1, waiting for transfers between devices, shards(): lax.psum_scatter(totals[7].astype(jnp.bfloat16), 'dp', scatter_dimension=...  141 us
    unnamed x3, blocking collectives  133 us
    dot_general x10, matrix products, row_product(): lax.dot_general(left, right, (((0,), (0,)), ((), ())), preferred_element_...  110 us
    all_gather x1, waiting for transfers between devices, shards(): lax.all_gather(up_weight, 'dp', axis=0, tiled=True)  98.3 us
    all_gather x1, waiting for transfers between devices, shards(): lax.all_gather(gene_weight, 'dp', axis=0, tiled=True)  97.8 us
    all_gather x1, waiting for transfers between devices, shards(): lax.all_gather(down_weight, 'dp', axis=0, tiled=True)  96.1 us
  transfers between devices with their start and end apart: 13, of which 11 were waited for; matrix products, arithmetic and copies ran while one was open for 19% of the time, Pallas kernels for 0%

commit v1 on v0

--- a/solution.py
+++ b/solution.py
@@ -306,7 +306,7 @@
         lax.psum(owned[5].astype(jnp.bfloat16), "query").astype(jnp.float32),
         lax.psum(owned[6].astype(jnp.bfloat16), "query").astype(jnp.float32),
         lax.psum(owned[7].astype(jnp.bfloat16), "query").astype(jnp.float32),
-        lax.psum(owned[8].astype(jnp.bfloat16), "query").astype(jnp.float32),
+        jnp.sum(lax.all_gather(owned[8].astype(jnp.bfloat16), "query"), axis=0).astype(jnp.float32),
         lax.psum(owned[9].astype(jnp.bfloat16), "query").astype(jnp.float32),
         lax.psum(owned[10].astype(jnp.bfloat16), "query").astype(jnp.float32),
     )

time: 1560 us -> 1560 us (level)
    unnamed x222 -> x214, local copies, waits for them, and re-layouts: 34.9 us -> 31 us
  transfers between devices with their start and end apart: 13 -> 14, of which waited for: 11 -> 11; matrix products, arithmetic and copies ran while one was open for 19% -> 19% of each run, Pallas kernels for 0% -> 0%
where the time goes in v1:
time: 1560 us; the launch traced here: 1550 us
  waiting for transfers between devices  964 us (62%)
  matrix products  342 us (22%)
  blocking collectives  147 us (9%)
  other arithmetic  37.6 us (2%)
  local copies, waits for them, and re-layouts  37.2 us (2%)
  between operations  18 us (1%)
    reduce_scatter x1, waiting for transfers between devices, shards(): lax.psum_scatter(totals[7].astype(jnp.bfloat16), 'dp', scatter_dimension=...  142 us
    reduce_scatter x1, waiting for transfers between devices, shards(): lax.psum_scatter(totals[3].astype(jnp.bfloat16), 'dp', scatter_dimension=...  142 us
    reduce_scatter x1, waiting for transfers between devices, shards(): lax.psum_scatter(totals[2].astype(jnp.bfloat16), 'dp', scatter_dimension=...  141 us
    unnamed x3, blocking collectives  133 us
    dot_general x10, matrix products, row_product(): lax.dot_general(left, right, (((0,), (0,)), ((), ())), preferred_element_...  113 us
    all_gather x1, waiting for transfers between devices, shards(): lax.all_gather(up_weight, 'dp', axis=0, tiled=True)  98.3 us
    all_gather x1, waiting for transfers between devices, shards(): lax.all_gather(gene_weight, 'dp', axis=0, tiled=True)  97.8 us
    all_gather x1, waiting for transfers between devices, shards(): lax.all_gather(down_weight, 'dp', axis=0, tiled=True)  96.1 us
  transfers between devices with their start and end apart: 14, of which 11 were waited for; matrix products, arithmetic and copies ran while one was open for 19% of the time, Pallas kernels for 0%

profile of v1, /device:TPU:0, one launch (start us, length us, event | category | flops | bytes accessed | tf_op | source)
XLA Modules:
  0.0 1547.1 jit_solution(2406345532875629870)
XLA Ops:
  14.5 65.3 %all-reduce.13 = (bf16[1280]{0:T(1024)(128)(2,1)S(1)}, bf16[5120]{0:T(1024)(128)(2,1)S(1)}, bf16[1280]{0:T(1024)(128)(2,1)S(1)}, bf16[5120]{0:T(1024)(128)(2,1)S(1)}, bf16[5120]{0:T(1024)(128)(2,1)S(1)}) all-reduce(bf16[1280]{0:T(1024)(128)(2,1)S(1)} %dynamic-update-slice.6, ...), channel_id=1, replica_groups=mesh['dp'=16,'query'=2] {'dp'}, use_global_device_ids=true, to_apply=%add | all-reduce | flops 17920 | bytes 71680
  81.0 16.6 %all-gather.11.cloned.1.call-done = bf16[1280,3840]{1,0:T(8,128)(2,1)} async-done(((bf16[80,3840]{1,0:T(8,128)(2,1)}), bf16[1280,3840]{1,0:T(8,128)(2,1)}) %all-gather.11.cloned.1.call-update) | async-done | bytes 9830416 | tf_op jit(solution)/shard_map/all_gather | solution.py:222
  97.6 5.3 convolution_convert_fusion
  103.7 5.9 convolution_convert_fusion.1
  112.9 31.2 %all-gather.13.cloned.1.call-done = bf16[1280,1280]{1,0:T(8,128)(2,1)} async-done(((bf16[80,1280]{1,0:T(8,128)(2,1)}), bf16[1280,1280]{1,0:T(8,128)(2,1)}) %all-gather.13.cloned.1.call-update) | async-done | bytes 3276816 | tf_op jit(solution)/shard_map/all_gather | solution.py:223
  151.0 98.3 %all-gather.15.cloned.1.call-done = bf16[1280,5120]{1,0:T(8,128)(2,1)} async-done(((bf16[80,5120]{1,0:T(8,128)(2,1)}), bf16[1280,5120]{1,0:T(8,128)(2,1)}) %all-gather.15.cloned.1.call-update) | async-done | bytes 13107216 | tf_op jit(solution)/shard_map/all_gather | solution.py:224
  249.3 8.2 convolution_add_fusion.1
  257.5 96.1 %all-gather.17.cloned.1.call-done = bf16[5120,1280]{1,0:T(8,128)(2,1)} async-done(((bf16[320,1280]{1,0:T(8,128)(2,1)}), bf16[5120,1280]{1,0:T(8,128)(2,1)}) %all-gather.17.cloned.1.call-update) | async-done | bytes 13107216 | tf_op jit(solution)/shard_map/all_gather | solution.py:225
  353.6 8.0 fusion.27
  361.6 4.7 all-gather.2
  370.8 4.4 all-gather.1
  375.1 82.8 %all-gather.19.cloned.1.call-done = bf16[1280,5120]{1,0:T(8,128)(2,1)} async-done(((bf16[80,5120]{1,0:T(8,128)(2,1)}), bf16[1280,5120]{1,0:T(8,128)(2,1)}) %all-gather.19.cloned.1.call-update) | async-done | bytes 13107216 | tf_op jit(solution)/shard_map/all_gather | solution.py:229
  457.9 6.5 fusion.165
  464.5 97.8 %all-gather.21.cloned.1.call-done = bf16[1280,5120]{1,0:T(8,128)(2,1)} async-done(((bf16[80,5120]{1,0:T(8,128)(2,1)}), bf16[1280,5120]{1,0:T(8,128)(2,1)}) %all-gather.21.cloned.1.call-update) | async-done | bytes 13107216 | tf_op jit(solution)/shard_map/all_gather | solution.py:230
  562.3 10.4 fusion.49
  572.7 6.2 add_add_fusion
  579.0 12.6 fusion.53
  593.5 9.9 multiply_reduce_fusion.3
  604.7 11.1 convert_reduce_fusion.1
  615.8 12.7 fusion.51
  628.5 16.2 %fusion.2 = bf16[1280,5120]{0,1:T(8,128)(2,1)} fusion(f32[5120,1280]{1,0:T(8,128)} %fusion.51, bf16[384,5120]{1,0:T(8,128)(2,1)} %get-tuple-element.136, bf16[2,1,384,1280]{3,2,1,0:T(8,128)(2,1)} %param.34), kind=kOutput, calls=%fused_computation.7 | convolution fusion | flops 5046272000 | bytes 44236800 | tf_op jit(solution)/shard_map/dot_general | solution.py:14
  644.7 17.6 %copy.88 = bf16[1280,5120]{1,0:T(8,128)(2,1)} copy(bf16[1280,5120]{0,1:T(8,128)(2,1)} %fusion.2) | data formatting | bytes 26214400
  670.3 14.1 convolution_convert_fusion.5
  684.4 13.5 convolution_convert_fusion.4
  697.9 8.3 all-reduce.15
  708.8 11.2 convert_reduce_fusion.3
  720.0 10.6 multiply_reduce_fusion.7
  730.6 9.7 convert_reduce_fusion.2
  740.4 10.3 multiply_reduce_fusion.6
  771.6 3.2 convolution_bitcast_fusion.4
  777.3 3.1 convolution_bitcast_fusion.2
  786.1 8.4 fusion.116
  794.5 11.1 add_convert_fusion.4
  806.7 13.3 fusion.146
  820.0 15.7 %add_convert_fusion.2 = bf16[5120,1280]{1,0:T(8,128)(2,1)} fusion(f32[5120,1280]{1,0:T(8,128)} %fusion.146, f32[128,1280]{1,0:T(8,128)S(1)} %copy-done.22, f32[128,5120]{1,0:T(8,128)} %convolution_add_fusion.1), kind=kOutput, calls=%fused_computation.4 | convolution fusion | flops 1696890880 | bytes 42598400 | tf_op jit(solution)/shard_map/dot_general | solution.py:14
  836.4 13.8 fusion.167
  850.3 17.7 %add_convert_fusion.1 = bf16[1280,5120]{1,0:T(8,128)(2,1)} fusion(f32[1280,5120]{1,0:T(8,128)} %fusion.167, f32[2,5120]{1,0:T(2,128)S(1)} %fusion.134, bf16[2,1,1280]{2,1,0:T(2,128)(2,1)S(1)} %copy-done.58), kind=kOutput, calls=%fused_computation.3 | convolution fusion | flops 170393600 | bytes 39367680 | tf_op jit(solution)/shard_map/dot_general | solution.py:188
  869.1 13.0 fusion.185
  882.0 18.8 %add_convert_fusion.3 = bf16[1280,5120]{1,0:T(8,128)(2,1)} fusion(f32[1280,5120]{1,0:T(8,128)} %fusion.185, bf16[128,5120]{1,0:T(8,128)(2,1)} %copy-done.26, f32[128,1280]{1,0:T(8,128)S(1)} %copy-done.6, f32[128]{0:T(128)S(1)} %copy-done.72, f32[128]{0:T(128)S(1)} %copy-done.67, f32[1280]{0:T(1024)S(1)} %convert_element_type.333), kind=kOutput, calls=%fused_computation.5 | convolution fusion | flops 1691484160 | bytes 41293824 | tf_op jit(solution)/shard_map/dot_general | solution.py:14
  902.9 8.8 fusion.194
  911.7 75.1 %reduce-scatter.9.cloned.1.call-done = bf16[80,3840]{1,0:T(8,128)(2,1)} async-done(((bf16[1280,3840]{1,0:T(8,128)(2,1)}), bf16[80,3840]{1,0:T(8,128)(2,1)}) %reduce-scatter.9.cloned.1.call-update) | async-done | bytes 614416 | tf_op jit(solution)/shard_map/reduce_scatter | solution.py:266
  986.8 142.1 %reduce-scatter.15.cloned.1.call-done = bf16[320,1280]{1,0:T(8,128)(2,1)} async-done(((bf16[5120,1280]{1,0:T(8,128)(2,1)}), bf16[320,1280]{1,0:T(8,128)(2,1)}) %reduce-scatter.15.cloned.1.call-update) | async-done | bytes 819216 | tf_op jit(solution)/shard_map/reduce_scatter | solution.py:275
  1128.9 142.2 %reduce-scatter.17.cloned.1.call-done = bf16[80,5120]{1,0:T(8,128)(2,1)} async-done(((bf16[1280,5120]{1,0:T(8,128)(2,1)}), bf16[80,5120]{1,0:T(8,128)(2,1)}) %reduce-scatter.17.cloned.1.call-update) | async-done | bytes 819216 | tf_op jit(solution)/shard_map/reduce_scatter | solution.py:287
  1271.1 141.5 %reduce-scatter.13.cloned.1.call-done = bf16[80,5120]{1,0:T(8,128)(2,1)} async-done(((bf16[1280,5120]{1,0:T(8,128)(2,1)}), bf16[80,5120]{1,0:T(8,128)(2,1)}) %reduce-scatter.13.cloned.1.call-update) | async-done | bytes 819216 | tf_op jit(solution)/shard_map/reduce_scatter | solution.py:272
  1412.7 8.3 fusion.81
  1421.1 59.6 %all-reduce.12 = (bf16[1280]{0:T(1024)(128)(2,1)S(1)}, bf16[1280]{0:T(1024)(128)(2,1)S(1)}, bf16[5120]{0:T(1024)(128)(2,1)S(1)}, bf16[5120]{0:T(1024)(128)(2,1)S(1)}, bf16[5120]{0:T(1024)(128)(2,1)S(1)}) all-reduce(bf16[1280]{0:T(1024)(128)(2,1)S(1)} %add_convert_fusion.9, ...), channel_id=9, replica_groups=mesh['dp'=16,'query'=2] {'dp'}, use_global_device_ids=true, to_apply=%region_36.37.clone | all-reduce | flops 17920 | bytes 71680
  1481.1 5.0 all-reduce.14
  1496.9 36.4 %all-reduce.19.cloned.1.call-done = (bf16[80,3840]{1,0:T(8,128)(2,1)}, bf16[80,1280]{1,0:T(8,128)(2,1)}, bf16[80,5120]{1,0:T(8,128)(2,1)}, bf16[320,1280]{1,0:T(8,128)(2,1)}, bf16[80,5120]{1,0:T(8,128)(2,1)}) async-done(((bf16[80,3840]{1,0:T(8,128)(2,1)}, bf16[80,1280]{1,0:T(8,128)(2,1)}, bf16[80,5120]{1,0:T(8,128)(2,1)}, bf16[320,1280]{1,0:T(8,128)(2,1)}, bf16[80,5120]{1,0:T(8,128)(2,1)}), ...) | async-done | bytes 3276816 | tf_op jit(solution)/shard_map/psum | solution.py:301
  (332 shorter events, 86.5 us)
Async XLA Ops:
  7.2 72.5 %copy-start.82 = (s32[1,2,1]{1,2,0:T(1,128)S(1)}, s32[1,2,1]{1,2,0:T(1,128)}, u32[]{:S(2)}) copy-start(s32[1,2,1]{1,2,0:T(1,128)} %param.37) | copy-start | bytes 28
  7.3 73.1 %copy-start.79 = (s32[2,1,384]{2,1,0:T(1,128)S(1)}, s32[2,1,384]{2,1,0:T(1,128)}, u32[]{:S(2)}) copy-start(s32[2,1,384]{2,1,0:T(1,128)} %param.35) | copy-start | bytes 9220
  7.3 73.1 %copy-start.80 = (s32[2,1,384]{2,1,0:T(1,128)S(1)}, s32[2,1,384]{2,1,0:T(1,128)}, u32[]{:S(2)}) copy-start(s32[2,1,384]{2,1,0:T(1,128)} %param.36) | copy-start | bytes 9220
  7.3 73.2 %copy-start.7 = (bf16[2,1,128,1280]{3,2,1,0:T(8,128)(2,1)S(1)}, bf16[2,1,128,1280]{3,2,1,0:T(8,128)(2,1)}, u32[]{:S(2)}) copy-start(bf16[2,1,128,1280]{3,2,1,0:T(8,128)(2,1)} %param.21) | copy-start | bytes 1966084
  7.3 90.3 %all-gather.11.cloned.1.call-start = ((), (), s32[]{:S(2)}) async-start(), calls=%async_computation.6 | async-start | bytes 10444800 | tf_op jit(solution)/shard_map/all_gather | solution.py:222
  8.0 136.1 %all-gather.13.cloned.1.call-start = ((), (), s32[]{:S(2)}) async-start(), calls=%async_computation.7 | async-start | bytes 3481600 | tf_op jit(solution)/shard_map/all_gather | solution.py:223
  8.8 240.5 %all-gather.15.cloned.1.call-start = ((), (), s32[]{:S(2)}) async-start(), calls=%async_computation.8 | async-start | bytes 13926400 | tf_op jit(solution)/shard_map/all_gather | solution.py:224
  9.5 344.1 %all-gather.17.cloned.1.call-start = ((), (), s32[]{:S(2)}) async-start(), calls=%async_computation.9 | async-start | bytes 13926400 | tf_op jit(solution)/shard_map/all_gather | solution.py:225
  10.1 447.9 %all-gather.19.cloned.1.call-start = ((), (), s32[]{:S(2)}) async-start(), calls=%async_computation.10 | async-start | bytes 13926400 | tf_op jit(solution)/shard_map/all_gather | solution.py:229
  10.7 551.6 %all-gather.21.cloned.1.call-start = ((), (), s32[]{:S(2)}) async-start(), calls=%async_computation.11 | async-start | bytes 13926400 | tf_op jit(solution)/shard_map/all_gather | solution.py:230
  11.2 889.6 %reduce-scatter.19.cloned.1.call-start = ((), (), s32[]{:S(2)}) async-start(), calls=%async_computation.18 | async-start | bytes 13926400 | tf_op jit(solution)/shard_map/reduce_scatter | solution.py:290
  79.8 23.9 %copy-start.41 = (f32[1280]{0:T(1024)}, f32[1280]{0:T(1024)S(1)}, u32[]{:S(2)}) copy-start(f32[1280]{0:T(1024)S(1)} %convert_element_type.327) | copy-start | bytes 15364
  80.6 22.3 %copy-start.73 = (f32[128]{0:T(128)}, f32[128]{0:T(128)S(1)}, u32[]{:S(2)}) copy-start(f32[128]{0:T(128)S(1)} %get-tuple-element.158) | copy-start | bytes 1540
  80.6 23.0 %copy-start.68 = (f32[128]{0:T(128)}, f32[128]{0:T(128)S(1)}, u32[]{:S(2)}) copy-start(f32[128]{0:T(128)S(1)} %get-tuple-element.159) | copy-start | bytes 1540
  81.0 22.0 %copy-start.77 = (f32[128]{0:T(128)}, f32[128]{0:T(128)S(1)}, u32[]{:S(2)}) copy-start(f32[128]{0:T(128)S(1)} %add_rsqrt_fusion.1) | copy-start | bytes 1540
  81.0 22.6 %copy-start.75 = (f32[128]{0:T(128)}, f32[128]{0:T(128)S(1)}, u32[]{:S(2)}) copy-start(f32[128]{0:T(128)S(1)} %add_rsqrt_fusion.3) | copy-start | bytes 1540
  112.9 34.2 %copy-start.36 = (bf16[20,64,128]{2,1,0:T(8,128)(2,1)}, bf16[20,64,128]{2,1,0:T(8,128)(2,1)S(1)}, u32[]{:S(2)}) copy-start(bf16[20,64,128]{2,1,0:T(8,128)(2,1)S(1)} %convolution_convert_fusion.6) | copy-start | bytes 983044
  146.8 605.0 %copy-start.5 = (f32[128,1280]{1,0:T(8,128)}, f32[128,1280]{1,0:T(8,128)S(1)}, u32[]{:S(2)}) copy-start(f32[128,1280]{1,0:T(8,128)S(1)} %get-tuple-element.145) | copy-start | bytes 1966084
  146.8 102.5 %copy-start.66 = (f32[128]{0:T(128)}, f32[128]{0:T(128)S(1)}, u32[]{:S(2)}) copy-start(f32[128]{0:T(128)S(1)} %broadcast_multiply_fusion.8) | copy-start | bytes 1540
  150.7 589.6 %copy-start.9 = (f32[128,1280]{1,0:T(8,128)}, f32[128,1280]{1,0:T(8,128)S(1)}, u32[]{:S(2)}) copy-start(f32[128,1280]{1,0:T(8,128)S(1)} %get-tuple-element.149) | copy-start | bytes 1966084
  151.0 106.5 %copy-start.71 = (f32[128]{0:T(128)}, f32[128]{0:T(128)S(1)}, u32[]{:S(2)}) copy-start(f32[128]{0:T(128)S(1)} %add_rsqrt_fusion) | copy-start | bytes 1540
  353.6 12.7 copy-start
  353.6 14.7 slice-start.4
  353.6 14.7 slice-start.5
  353.6 14.7 slice-start.6
  366.3 91.6 %copy-start.57 = (bf16[2,1,1280]{2,1,0:T(2,128)(2,1)}, bf16[2,1,1280]{2,1,0:T(2,128)(2,1)S(1)}, u32[]{:S(2)}) copy-start(bf16[2,1,1280]{2,1,0:T(2,128)(2,1)S(1)} %all-gather.2) | copy-start | bytes 15364
  370.8 93.7 %copy-start.45 = (bf16[128,1280]{1,0:T(8,128)(2,1)}, bf16[128,1280]{1,0:T(8,128)(2,1)S(1)}, u32[]{:S(2)}) copy-start(bf16[128,1280]{1,0:T(8,128)(2,1)S(1)} %fusion.26) | copy-start | bytes 983044
  375.1 216.5 %copy-start.59 = (bf16[2,1,1280]{2,1,0:T(2,128)(2,1)}, bf16[2,1,1280]{2,1,0:T(2,128)(2,1)S(1)}, u32[]{:S(2)}) copy-start(bf16[2,1,1280]{2,1,0:T(2,128)(2,1)S(1)} %all-gather.1) | copy-start | bytes 15364
  572.7 18.9 %slice-start = ((s8[13107200]{0:T(1024)(128)(4,1)}), s8[4194304]{0:T(1024)(128)(4,1)S(1)}, s32[]{:S(2)}) async-start(s8[13107200]{0:T(1024)(128)(4,1)} %bitcast.252), calls=%async_computation.20 | async-start | bytes 8388608
  572.7 18.9 %slice-start.1 = ((s8[13107200]{0:T(1024)(128)(4,1)}), s8[4194304]{0:T(1024)(128)(4,1)S(1)}, s32[]{:S(2)}) async-start(s8[13107200]{0:T(1024)(128)(4,1)} %bitcast.252), calls=%async_computation.21 | async-start | bytes 8388608
  579.0 12.7 slice-start.2
  615.8 12.7 copy-start.4
  662.4 249.4 %reduce-scatter.11.cloned.1.call-start = ((), (), s32[]{:S(2)}) async-start(), calls=%async_computation.13 | async-start | bytes 3481600 | tf_op jit(solution)/shard_map/reduce_scatter | solution.py:269
  707.8 44.0 %copy-start.21 = (f32[128,1280]{1,0:T(8,128)}, f32[128,1280]{1,0:T(8,128)S(1)}, u32[]{:S(2)}) copy-start(f32[128,1280]{1,0:T(8,128)S(1)} %scatter-add.9) | copy-start | bytes 1966084
  708.8 31.6 %copy-start.23 = (f32[128,1280]{1,0:T(8,128)}, f32[128,1280]{1,0:T(8,128)S(1)}, u32[]{:S(2)}) copy-start(f32[128,1280]{1,0:T(8,128)S(1)} %scatter-add.6) | copy-start | bytes 1966084
  755.7 231.0 %reduce-scatter.9.cloned.1.call-start = ((), (), s32[]{:S(2)}) async-start(), calls=%async_computation.12 | async-start | bytes 10444800 | tf_op jit(solution)/shard_map/reduce_scatter | solution.py:266
  805.6 14.4 copy-start.22
  805.6 323.3 %reduce-scatter.15.cloned.1.call-start = ((), (), s32[]{:S(2)}) async-start(), calls=%async_computation.15 | async-start | bytes 13926400 | tf_op jit(solution)/shard_map/reduce_scatter | solution.py:275
  835.7 14.5 copy-start.58
  835.8 435.3 %reduce-scatter.17.cloned.1.call-start = ((), (), s32[]{:S(2)}) async-start(), calls=%async_computation.16 | async-start | bytes 13926400 | tf_op jit(solution)/shard_map/reduce_scatter | solution.py:287
  868.0 14.0 copy-start.6
  868.0 544.5 %reduce-scatter.13.cloned.1.call-start = ((), (), s32[]{:S(2)}) async-start(), calls=%async_computation.14 | async-start | bytes 13926400 | tf_op jit(solution)/shard_map/reduce_scatter | solution.py:272
  900.8 592.8 %all-gather.23.cloned.1.call-start = ((), (), s32[]{:S(2)}) async-start(), calls=%async_computation.17 | async-start | bytes 2457600 | tf_op jit(solution)/shard_map/all_gather | solution.py:309
  901.6 631.7 %all-reduce.19.cloned.1.call-start = ((), (), s32[]{:S(2)}) async-start(), calls=%async_computation.19 | async-start | bytes 6553600 | tf_op jit(solution)/shard_map/psum | solution.py:301
  911.7 500.8 %copy-start.28 = (bf16[128,3,20,64]{0,3,2,1:T(8,128)(2,1)S(1)}, bf16[128,3,20,64]{0,3,2,1:T(8,128)(2,1)}, u32[]{:S(2)}) copy-start(bf16[128,3,20,64]{0,3,2,1:T(8,128)(2,1)} %copy-done.27) | copy-start | bytes 2949124
  1412.6 76.2 %copy-start.44 = (bf16[128,1280]{1,0:T(8,128)(2,1)S(1)}, bf16[128,1280]{1,0:T(8,128)(2,1)}, u32[]{:S(2)}) copy-start(bf16[128,1280]{1,0:T(8,128)(2,1)} %copy-done.43) | copy-start | bytes 983044
  1412.6 78.1 %copy-start.18 = (f32[128,1280]{1,0:T(8,128)S(1)}, f32[128,1280]{1,0:T(8,128)}, u32[]{:S(2)}) copy-start(f32[128,1280]{1,0:T(8,128)} %copy-done.17) | copy-start | bytes 1966084
  1412.7 78.1 %copy-start.20 = (f32[128,1280]{1,0:T(8,128)S(1)}, f32[128,1280]{1,0:T(8,128)}, u32[]{:S(2)}) copy-start(f32[128,1280]{1,0:T(8,128)} %copy-done.19) | copy-start | bytes 1966084
  (63 other events, 286.8 us)
Sparse Core Ops, SparseCore 0:
  10.4 87.1 all-gather.10
  99.9 44.1 all-gather.12
  146.4 102.8 all-gather.14
  251.4 102.1 all-gather.16
  355.7 102.1 all-gather.18
  460.1 102.1 all-gather.20
  662.5 136.5 reduce-scatter.18
  803.4 65.9 reduce-scatter.10
  873.5 113.2 reduce-scatter.8
  990.7 138.1 reduce-scatter.14
  1133.6 137.4 reduce-scatter.16
  1275.0 137.4 reduce-scatter.12
  1414.1 27.0 all-gather.22
  1443.8 89.4 all-reduce.18
